TPU v7x, 32 devices: a whole 2x2x4 slice. The times are simulated.
32 devices in a mesh: dp: 2 (over core), expert: 16 (over z, y, x).
Axes of the slice: x: 2, y: 2, z: 4, core: 2. Of those that a mesh axis runs over, the one named last changes fastest.
Arguments:
- tokens: bfloat16 [2048, 2048], P('expert'), may hold values from -6 to 6
- out_grad: bfloat16 [2048, 2048], P('expert'), may hold values from -6 to 6
- route_ids: int32 [2048, 8], P('expert'), may hold values from 0 to 15, all different within a row; in each aligned block of 128 rows (0 to 127, 128 to 255, ...) at most 72 rows name the same one
- route_probs: float32 [2048, 8], P('expert'), may hold values from 0.05 to 1
- gate_store: bfloat16 [16, 2048, 768], P(None, 'expert', 'dp'), may hold values from -0.125 to 0.125
- up_store: bfloat16 [16, 2048, 768], P(None, 'expert', 'dp'), may hold values from -0.125 to 0.125
- down_store: bfloat16 [16, 2048, 768], P(None, 'expert', 'dp'), may hold values from -0.21875 to 0.21875
Outputs:
- grad_gate: bfloat16 [16, 2048, 768], P('expert', None, 'dp')
- grad_up: bfloat16 [16, 2048, 768], P('expert', None, 'dp')
- grad_down: bfloat16 [16, 2048, 768], P('expert', None, 'dp')
- grad_tokens: bfloat16 [2048, 2048], P('expert')
Inputs may be any that keep to these rules, and one draw needn't show every extreme that they name: `route_ids`: among the 128 tokens of one device no expert is named more than 72 times, and in every draw some expert is named exactly 72 times by some device's tokens.
All inputs are finite; a program needn't handle non-finite values.
Results may differ from a plain program's by a relative error of at most 0.0065.
Values may be sent and summed in bfloat16 or wider, within the bound.
A program may use at most 128 MiB of HBM per device.

v0:
```python
import jax
import jax.numpy as jnp
from jax import lax
from jax.sharding import PartitionSpec as P


def joined(own, other):
    first = lax.axis_index("dp") == 0
    return jnp.where(first, jnp.concatenate([own, other], -1), jnp.concatenate([other, own], -1))


def swapped(part):
    return lax.ppermute(part, "dp", [(0, 1), (1, 0)])


def placed(tokens, out_grad, route_ids, route_probs, gate_store, up_store, down_store):
    tok_rows, model_width = tokens.shape
    top_count = route_ids.shape[1]
    experts = lax.axis_size("expert")
    capacity = max(2, 9 * tok_rows * top_count // (8 * experts))
    slots = experts * capacity
    width = model_width // 2
    here = lax.axis_index("dp") * width
    there = width - here
    f32, bf16 = (jnp.float32, jnp.bfloat16)
    chosen = route_ids[:, :, None] == jnp.arange(experts, dtype=jnp.int32)[None, None, :]
    weight = jnp.sum(jnp.where(chosen, route_probs[:, :, None], 0.0), axis=1)
    named = jnp.any(chosen, axis=1)
    earlier = jnp.arange(tok_rows)[:, None] > jnp.arange(tok_rows)[None, :]
    rank = jnp.dot(earlier.astype(bf16), named.astype(bf16), preferred_element_type=f32)
    rank = jnp.where(named, rank, -1.0)
    hit = rank.T[:, None, :] == jnp.arange(capacity, dtype=f32)[None, :, None]
    slot_prob = jnp.sum(jnp.where(hit, weight.T[:, None, :], 0.0), axis=2)
    place = hit.astype(bf16).reshape(slots, tok_rows)
    x_part = jnp.dot(
        place, lax.dynamic_slice_in_dim(tokens, here, width, 1), preferred_element_type=f32
    ).astype(bf16)
    dy_part = (
        jnp.dot(
            place, lax.dynamic_slice_in_dim(out_grad, here, width, 1), preferred_element_type=f32
        )
        * slot_prob.reshape(slots, 1)
    ).astype(bf16)

    def exchange(a):
        return lax.all_to_all(a, "expert", split_axis=0, concat_axis=0, tiled=True)

    def panel(store):
        return lax.all_to_all(store, "expert", split_axis=0, concat_axis=1, tiled=True)[0]

    x_own = exchange(x_part.reshape(experts, capacity, width)).reshape(slots, width)
    gate_panel = panel(gate_store)
    up_panel = panel(up_store)
    dy_own = exchange(dy_part.reshape(experts, capacity, width)).reshape(slots, width)
    down_panel = panel(down_store)
    rows_in = joined(x_own, swapped(x_own))
    dy_rows = joined(dy_own, swapped(dy_own))
    gate_pre = jnp.dot(rows_in, gate_panel, preferred_element_type=f32)
    up_pre = jnp.dot(rows_in, up_panel, preferred_element_type=f32)
    sig = jax.nn.sigmoid(gate_pre)
    activation = (gate_pre * sig * up_pre).astype(bf16)
    act_grad = jnp.dot(dy_rows, down_panel, preferred_element_type=f32)
    up_grad = (act_grad * gate_pre * sig).astype(bf16)
    gate_grad = (act_grad * up_pre * sig * (1.0 + gate_pre * (1.0 - sig))).astype(bf16)
    back = (((1,), (1,)), ((), ()))

    def slot_part(start):
        rows = [lax.dynamic_slice_in_dim(w, start, width, 0) for w in (gate_panel, up_panel)]
        return lax.dot_general(
            gate_grad, rows[0], back, preferred_element_type=f32
        ) + lax.dot_general(up_grad, rows[1], back, preferred_element_type=f32)

    arrived = swapped(slot_part(there).astype(bf16))
    summed = (slot_part(here) + arrived.astype(f32)).astype(bf16)
    returned = exchange(summed.reshape(experts, capacity, width)).reshape(slots, width)
    share = lax.dot_general(
        place, returned, (((0,), (0,)), ((), ())), preferred_element_type=f32
    ).astype(bf16)
    grad_tokens = joined(share, swapped(share))
    outer = (((0,), (0,)), ((), ()))
    grad_down = lax.dot_general(dy_rows, activation, outer, preferred_element_type=f32).astype(bf16)
    grad_gate = lax.dot_general(rows_in, gate_grad, outer, preferred_element_type=f32).astype(bf16)
    grad_up = lax.dot_general(rows_in, up_grad, outer, preferred_element_type=f32).astype(bf16)
    return (grad_gate[None], grad_up[None], grad_down[None], grad_tokens)


def solution(mesh):
    return jax.shard_map(
        placed,
        mesh=mesh,
        in_specs=(
            P("expert", None),
            P("expert", None),
            P("expert", None),
            P("expert", None),
            P(None, "expert", "dp"),
            P(None, "expert", "dp"),
            P(None, "expert", "dp"),
        ),
        out_specs=(
            P("expert", None, "dp"),
            P("expert", None, "dp"),
            P("expert", None, "dp"),
            P("expert", None),
        ),
        check_vma=False,
    )
```

profile of v0, /device:TPU:15, one launch (start us, length us, event | category | flops | bytes accessed | tf_op | source)
XLA Modules:
  0.0 329.0 jit_solution(13981634180581247777)
XLA Ops:
  0.6 0.0 copy-start
  0.6 41.9 %all_to_all.42 = bf16[16,128,384]{2,1,0:T(8,128)(2,1)} all-to-all(bf16[16,128,384]{2,1,0:T(8,128)(2,1)} %param.11), channel_id=1, replica_groups=mesh['dp'=2,'expert'=16] {'expert'}, dimensions={0} | all-to-all | bytes 3145728 | tf_op jit(solution)/shard_map/all_to_all | solution.py:49
  42.5 5.9 %all-to-all-start.3 = ((bf16[16,128,384]{2,1,0:T(8,128)(2,1)}), bf16[16,128,384]{2,1,0:T(8,128)(2,1)S(1)}, u32[]{:S(2)}, u32[]{:S(2)}) async-start(bf16[16,128,384]{2,1,0:T(8,128)(2,1)} %param.12), calls=%async_computation.3 | async-start | bytes 3145728 | tf_op jit(solution)/shard_map/all_to_all | solution.py:49
  48.4 0.1 eq.49
  48.5 0.0 copy-done.6
  48.5 0.1 convolution_select_fusion
  48.7 0.2 bitcast_compare_fusion
  48.9 0.0 copy-done
  48.9 2.2 convolution_convert_fusion
  51.1 33.7 %all-to-all-done.3 = bf16[16,128,384]{2,1,0:T(8,128)(2,1)S(1)} async-done(((bf16[16,128,384]{2,1,0:T(8,128)(2,1)}), bf16[16,128,384]{2,1,0:T(8,128)(2,1)S(1)}, u32[]{:S(2)}, u32[]{:S(2)}) %all-to-all-start.3) | async-done | bytes 1572896 | tf_op jit(solution)/shard_map/all_to_all | solution.py:49
  84.8 4.7 %all-to-all-start = ((bf16[16,72,1024]{2,1,0:T(8,128)(2,1)}), bf16[16,72,1024]{2,1,0:T(8,128)(2,1)}, u32[]{:S(2)}, u32[]{:S(2)}) async-start(bf16[16,72,1024]{2,1,0:T(8,128)(2,1)} %bitcast.2), calls=%async_computation | async-start | bytes 4718592 | tf_op jit(solution)/shard_map/all_to_all | solution.py:46
  89.5 0.0 copy-done.7
  89.5 0.3 select_reduce_fusion
  89.9 0.1 mul.38
  90.0 0.0 copy-done.5
  90.0 2.2 fusion
  92.2 50.3 %all-to-all-done = bf16[16,72,1024]{2,1,0:T(8,128)(2,1)} async-done(((bf16[16,72,1024]{2,1,0:T(8,128)(2,1)}), bf16[16,72,1024]{2,1,0:T(8,128)(2,1)}, u32[]{:S(2)}, u32[]{:S(2)}) %all-to-all-start) | async-done | bytes 2359328 | tf_op jit(solution)/shard_map/all_to_all | solution.py:46
  142.5 4.6 %all-to-all-start.1 = ((bf16[16,72,1024]{2,1,0:T(8,128)(2,1)}), bf16[16,72,1024]{2,1,0:T(8,128)(2,1)}, u32[]{:S(2)}, u32[]{:S(2)}) async-start(bf16[16,72,1024]{2,1,0:T(8,128)(2,1)} %bitcast.5), calls=%async_computation.1 | async-start | bytes 4718592 | tf_op jit(solution)/shard_map/all_to_all | solution.py:46
  147.1 2.2 collective-permute-start
  149.2 50.9 %all-to-all-done.1 = bf16[16,72,1024]{2,1,0:T(8,128)(2,1)} async-done(((bf16[16,72,1024]{2,1,0:T(8,128)(2,1)}), bf16[16,72,1024]{2,1,0:T(8,128)(2,1)}, u32[]{:S(2)}, u32[]{:S(2)}) %all-to-all-start.1) | async-done | bytes 2359328 | tf_op jit(solution)/shard_map/all_to_all | solution.py:46
  200.1 4.6 %all-to-all-start.2 = ((bf16[16,128,384]{2,1,0:T(8,128)(2,1)}), bf16[16,128,384]{2,1,0:T(8,128)(2,1)}, u32[]{:S(2)}, u32[]{:S(2)}) async-start(bf16[16,128,384]{2,1,0:T(8,128)(2,1)} %param.13), calls=%async_computation.2 | async-start | bytes 3145728 | tf_op jit(solution)/shard_map/all_to_all | solution.py:49
  204.7 2.2 collective-permute-start.1
  206.9 0.0 collective-permute-done
  206.9 8.1 %fusion.29 = f32[1152,384]{1,0:T(8,128)} fusion(bf16[2048,384]{1,0:T(8,128)(2,1)} %bitcast.40, bf16[1152,1024]{1,0:T(8,128)(2,1)} %collective-permute-done, bf16[1152,1024]{1,0:T(8,128)(2,1)} %bitcast.3, pred[]{:T(512)S(6)} %eq.42), kind=kOutput, calls=%fused_computation.50 | convolution fusion | flops 1833172992 | bytes 8060929 | tf_op jit(solution)/shard_map/dot_general | solution.py:58
  215.0 7.6 %fusion.30 = f32[1152,384]{1,0:T(8,128)} fusion(bf16[2048,384]{1,0:T(8,128)(2,1)S(1)} %bitcast.37, bf16[1152,1024]{1,0:T(8,128)(2,1)} %collective-permute-done, bf16[1152,1024]{1,0:T(8,128)(2,1)} %bitcast.3, pred[]{:T(512)S(6)} %eq.42), kind=kOutput, calls=%fused_computation.51 | convolution fusion | flops 1833172992 | bytes 8060929 | tf_op jit(solution)/shard_map/dot_general | solution.py:59
  222.5 18.1 %all-to-all-done.2 = bf16[16,128,384]{2,1,0:T(8,128)(2,1)} async-done(((bf16[16,128,384]{2,1,0:T(8,128)(2,1)}), bf16[16,128,384]{2,1,0:T(8,128)(2,1)}, u32[]{:S(2)}, u32[]{:S(2)}) %all-to-all-start.2) | async-done | bytes 1572896 | tf_op jit(solution)/shard_map/all_to_all | solution.py:49
  240.7 0.0 collective-permute-done.1
  240.7 7.5 %multiply_convert_fusion.1 = (bf16[1152,384]{1,0:T(8,128)(2,1)S(1)}, bf16[1152,384]{1,0:T(8,128)(2,1)S(1)}) fusion(f32[1152,384]{1,0:T(8,128)} %fusion.29, f32[1152,384]{1,0:T(8,128)} %fusion.30, bf16[2048,384]{1,0:T(8,128)(2,1)} %bitcast.7, bf16[1152,1024]{1,0:T(8,128)(2,1)} %collective-permute-done.1, bf16[1152,1024]{1,0:T(8,128)(2,1)} %bitcast.6, ...), kind=kOutput, calls=%fused_computation.16 | convolution fusion | flops 1838923776 | bytes 11599873 | tf_op jit(solution)/shard_map/dot_general | solution.py:62
  248.2 0.0 copy-start.1
  248.2 0.0 copy-start.4
  248.2 0.0 copy-done.3
  248.2 1.4 fusion.9
  249.7 1.5 fusion.1
  251.1 1.5 collective-permute-start.2
  252.6 0.0 copy-done.1
  252.6 1.4 fusion.14
  254.0 2.7 collective-permute-done.2
  256.7 2.9 add_convert_fusion
  259.7 5.0 %all-to-all-start.5 = ((bf16[16,72,1024]{2,1,0:T(8,128)(2,1)}), bf16[16,72,1024]{2,1,0:T(8,128)(2,1)S(1)}, u32[]{:S(2)}, u32[]{:S(2)}) async-start(bf16[16,72,1024]{2,1,0:T(8,128)(2,1)} %bitcast.36), calls=%async_computation.5 | async-start | bytes 4718592 | tf_op jit(solution)/shard_map/all_to_all | solution.py:46
  264.7 0.0 copy-start.9
  264.7 8.1 %fusion.3 = bf16[1,2048,384]{2,1,0:T(8,128)(2,1)} fusion(bf16[1152,384]{1,0:T(8,128)(2,1)} %copy-done.4, bf16[1152,1024]{1,0:T(8,128)(2,1)} %collective-permute-done, bf16[1152,1024]{1,0:T(8,128)(2,1)} %bitcast.3, pred[]{:T(512)S(6)} %eq.42), kind=kOutput, calls=%fused_computation.13 | convolution fusion | flops 1833959424 | bytes 7176193 | tf_op jit(solution)/shard_map/dot_general | solution.py:83
  272.8 8.1 %fusion.4 = bf16[1,2048,384]{2,1,0:T(8,128)(2,1)} fusion(f32[1152,384]{1,0:T(8,128)S(1)} %copy-done.9, f32[1152,384]{1,0:T(8,128)S(1)} %copy-done.8, bf16[1152,1024]{1,0:T(8,128)(2,1)} %collective-permute-done.1, bf16[1152,1024]{1,0:T(8,128)(2,1)} %bitcast.6, pred[]{:T(512)S(6)} %eq.42), kind=kOutput, calls=%fused_computation.14 | convolution fusion | flops 1836613632 | bytes 9830401 | tf_op jit(solution)/shard_map/dot_general | solution.py:81
  280.9 37.3 %all-to-all-done.5 = bf16[16,72,1024]{2,1,0:T(8,128)(2,1)S(1)} async-done(((bf16[16,72,1024]{2,1,0:T(8,128)(2,1)}), bf16[16,72,1024]{2,1,0:T(8,128)(2,1)S(1)}, u32[]{:S(2)}, u32[]{:S(2)}) %all-to-all-start.5) | async-done | bytes 2359328 | tf_op jit(solution)/shard_map/all_to_all | solution.py:46
  318.2 0.6 fusion.5
  318.8 1.5 collective-permute-start.3
  320.2 7.8 %fusion.2 = bf16[1,2048,384]{2,1,0:T(8,128)(2,1)} fusion(bf16[1152,384]{1,0:T(8,128)(2,1)S(1)} %copy-done.2, bf16[1152,1024]{1,0:T(8,128)(2,1)} %collective-permute-done, bf16[1152,1024]{1,0:T(8,128)(2,1)} %bitcast.3, pred[]{:T(512)S(6)} %eq.42), kind=kOutput, calls=%fused_computation.12 | convolution fusion | flops 1833959424 | bytes 7176193 | tf_op jit(solution)/shard_map/dot_general | solution.py:82
  328.1 0.0 collective-permute-done.3
  328.1 0.9 maximum_select_fusion.4
  (13 shorter events, 0.1 us)
Async XLA Ops:
  0.6 48.3 %copy-start = (bf16[128,2048]{1,0:T(8,128)(2,1)S(1)}, bf16[128,2048]{1,0:T(8,128)(2,1)}, u32[]{:S(2)}) copy-start(bf16[128,2048]{1,0:T(8,128)(2,1)} %param.7) | copy-start | bytes 1572868
  42.5 6.0 %copy-start.6 = (s32[128,8]{0,1:T(8,128)S(1)}, s32[128,8]{0,1:T(8,128)}, u32[]{:S(2)}) copy-start(s32[128,8]{0,1:T(8,128)} %param.9) | copy-start | bytes 12292
  42.5 42.3 %all-to-all-start.3 = ((bf16[16,128,384]{2,1,0:T(8,128)(2,1)}), bf16[16,128,384]{2,1,0:T(8,128)(2,1)S(1)}, u32[]{:S(2)}, u32[]{:S(2)}) async-start(bf16[16,128,384]{2,1,0:T(8,128)(2,1)} %param.12), calls=%async_computation.3 | async-start | bytes 3145728 | tf_op jit(solution)/shard_map/all_to_all | solution.py:49
  84.8 4.7 %copy-start.7 = (f32[128,8]{0,1:T(8,128)S(1)}, f32[128,8]{0,1:T(8,128)}, u32[]{:S(2)}) copy-start(f32[128,8]{0,1:T(8,128)} %param.10) | copy-start | bytes 12292
  84.8 5.2 %copy-start.5 = (bf16[128,2048]{1,0:T(8,128)(2,1)S(1)}, bf16[128,2048]{1,0:T(8,128)(2,1)}, u32[]{:S(2)}) copy-start(bf16[128,2048]{1,0:T(8,128)(2,1)} %param.8) | copy-start | bytes 1572868
  84.8 57.7 %all-to-all-start = ((bf16[16,72,1024]{2,1,0:T(8,128)(2,1)}), bf16[16,72,1024]{2,1,0:T(8,128)(2,1)}, u32[]{:S(2)}, u32[]{:S(2)}) async-start(bf16[16,72,1024]{2,1,0:T(8,128)(2,1)} %bitcast.2), calls=%async_computation | async-start | bytes 4718592 | tf_op jit(solution)/shard_map/all_to_all | solution.py:46
  142.5 57.6 %all-to-all-start.1 = ((bf16[16,72,1024]{2,1,0:T(8,128)(2,1)}), bf16[16,72,1024]{2,1,0:T(8,128)(2,1)}, u32[]{:S(2)}, u32[]{:S(2)}) async-start(bf16[16,72,1024]{2,1,0:T(8,128)(2,1)} %bitcast.5), calls=%async_computation.1 | async-start | bytes 4718592 | tf_op jit(solution)/shard_map/all_to_all | solution.py:46
  147.1 59.8 %collective-permute-start = (bf16[1152,1024]{1,0:T(8,128)(2,1)}, bf16[1152,1024]{1,0:T(8,128)(2,1)}, u32[]{:S(2)}, u32[]{:S(2)}) collective-permute-start(bf16[1152,1024]{1,0:T(8,128)(2,1)} %bitcast.3), channel_id=1, source_target_pairs={{0,16},{16,0},{1,17},{17,1},{2,18},{18,2},{3,19},{19,3},{4,20},{20... | collective-permute-start | bytes 7077896 | tf_op jit(solution)/shard_map/ppermute | solution.py:13
  200.1 40.5 %all-to-all-start.2 = ((bf16[16,128,384]{2,1,0:T(8,128)(2,1)}), bf16[16,128,384]{2,1,0:T(8,128)(2,1)}, u32[]{:S(2)}, u32[]{:S(2)}) async-start(bf16[16,128,384]{2,1,0:T(8,128)(2,1)} %param.13), calls=%async_computation.2 | async-start | bytes 3145728 | tf_op jit(solution)/shard_map/all_to_all | solution.py:49
  204.7 36.0 %collective-permute-start.1 = (bf16[1152,1024]{1,0:T(8,128)(2,1)}, bf16[1152,1024]{1,0:T(8,128)(2,1)}, u32[]{:S(2)}, u32[]{:S(2)}) collective-permute-start(bf16[1152,1024]{1,0:T(8,128)(2,1)} %bitcast.6), channel_id=1, source_target_pairs={{0,16},{16,0},{1,17},{17,1},{2,18},{18,2},{3,19},{19,3},{4,20},{20... | collective-permute-start | bytes 7077896 | tf_op jit(solution)/shard_map/ppermute | solution.py:13
  240.7 7.5 %copy-start.3 = (bf16[16,128,384]{2,1,0:T(8,128)(2,1)S(1)}, bf16[16,128,384]{2,1,0:T(8,128)(2,1)}, u32[]{:S(2)}) copy-start(bf16[16,128,384]{2,1,0:T(8,128)(2,1)} %all_to_all.42) | copy-start | bytes 4718596
  248.2 4.4 %copy-start.1 = (bf16[1152,384]{1,0:T(8,128)(2,1)}, bf16[1152,384]{1,0:T(8,128)(2,1)S(1)}, u32[]{:S(2)}) copy-start(bf16[1152,384]{1,0:T(8,128)(2,1)S(1)} %get-tuple-element.5) | copy-start | bytes 2654212
  248.2 8.5 %copy-start.4 = (bf16[1152,384]{1,0:T(8,128)(2,1)}, bf16[1152,384]{1,0:T(8,128)(2,1)S(1)}, u32[]{:S(2)}) copy-start(bf16[1152,384]{1,0:T(8,128)(2,1)S(1)} %get-tuple-element.4) | copy-start | bytes 2654212
  251.1 5.6 %collective-permute-start.2 = (bf16[1152,1024]{1,0:T(8,128)(2,1)S(1)}, bf16[1152,1024]{1,0:T(8,128)(2,1)S(1)}, u32[]{:S(2)}, u32[]{:S(2)}) collective-permute-start(bf16[1152,1024]{1,0:T(8,128)(2,1)S(1)} %fusion.1), channel_id=1, source_target_pairs={{0,16},{16,0},{1,17},{17,1},{2,18},{18,2},{3,19},{19,3},{4,20},{20... | collective-permute-start | bytes 7077896 | tf_op jit(solution)/shard_map/ppermute | solution.py:13
  259.7 58.5 %all-to-all-start.5 = ((bf16[16,72,1024]{2,1,0:T(8,128)(2,1)}), bf16[16,72,1024]{2,1,0:T(8,128)(2,1)S(1)}, u32[]{:S(2)}, u32[]{:S(2)}) async-start(bf16[16,72,1024]{2,1,0:T(8,128)(2,1)} %bitcast.36), calls=%async_computation.5 | async-start | bytes 4718592 | tf_op jit(solution)/shard_map/all_to_all | solution.py:46
  264.7 8.2 %copy-start.8 = (f32[1152,384]{1,0:T(8,128)S(1)}, f32[1152,384]{1,0:T(8,128)}, u32[]{:S(2)}) copy-start(f32[1152,384]{1,0:T(8,128)} %fusion.29) | copy-start | bytes 5308420
  264.7 8.2 %copy-start.9 = (f32[1152,384]{1,0:T(8,128)S(1)}, f32[1152,384]{1,0:T(8,128)}, u32[]{:S(2)}) copy-start(f32[1152,384]{1,0:T(8,128)} %fusion.30) | copy-start | bytes 5308420
  318.2 2.0 copy-start.2
  318.8 9.3 %collective-permute-start.3 = (bf16[128,1024]{1,0:T(8,128)(2,1)S(1)}, bf16[128,1024]{1,0:T(8,128)(2,1)S(1)}, u32[]{:S(2)}, u32[]{:S(2)}) collective-permute-start(bf16[128,1024]{1,0:T(8,128)(2,1)S(1)} %fusion.5), channel_id=1, source_target_pairs={{0,16},{16,0},{1,17},{17,1},{2,18},{18,2},{3,19},{19,3},{4,20},{20... | collective-permute-start | bytes 786440 | tf_op jit(solution)/shard_map/ppermute | solution.py:13
where the time goes:
time: 330 us; the launch traced here: 329 us
  waiting for transfers between devices  193 us (58%)
  matrix products  59.6 us (18%)
  blocking collectives  41.9 us (13%)
  starting transfers between devices  32 us (10%)
    all_to_all x3, waiting for transfers between devices, exchange(): return lax.all_to_all(a, 'expert', split_axis=0, concat_axis=0, tiled=True)  138 us
    all_to_all x2, waiting for transfers between devices, panel(): lax.all_to_all(store, 'expert', split_axis=0, concat_axis=1, tiled=True)[0]  51.8 us
    all_to_all x1, blocking collectives, panel(): lax.all_to_all(store, 'expert', split_axis=0, concat_axis=1, tiled=True)[0]  41.9 us
    all_to_all x3, starting transfers between devices, exchange(): return lax.all_to_all(a, 'expert', split_axis=0, concat_axis=0, tiled=True)  14.3 us
    all_to_all x2, starting transfers between devices, panel(): lax.all_to_all(store, 'expert', split_axis=0, concat_axis=1, tiled=True)[0]  10.4 us
    dot_general x1, matrix products, placed(): lax.dot_general(rows_in, up_grad, outer, preferred_element_type=f32)  8.14 us
    dot_general x1, matrix products, placed(): gate_pre = jnp.dot(rows_in, gate_panel, preferred_element_type=f32)  8.1 us
    dot_general x1, matrix products, placed(): lax.dot_general(dy_rows, activation, outer, preferred_element_type=f32)  8.06 us
  transfers between devices with their start and end apart: 9, of which 6 were waited for; matrix products, arithmetic and copies ran while one was open for 14% of the time, Pallas kernels for 0%

commit v1 on v0

--- a/solution.py
+++ b/solution.py
@@ -2,6 +2,11 @@
 import jax.numpy as jnp
 from jax import lax
 from jax.sharding import PartitionSpec as P
+from jax.lax import all_to_all, axis_size
+
+switch_floor = lambda a0: jnp.concatenate(
+    all_to_all(jnp.stack(jnp.split(a0, axis_size("expert"), 0), 0), "expert", 0, 0), 1
+)
 
 
 def joined(own, other):
@@ -46,7 +51,7 @@
         return lax.all_to_all(a, "expert", split_axis=0, concat_axis=0, tiled=True)
 
     def panel(store):
-        return lax.all_to_all(store, "expert", split_axis=0, concat_axis=1, tiled=True)[0]
+        return switch_floor(store)[0]
 
     x_own = exchange(x_part.reshape(experts, capacity, width)).reshape(slots, width)
     gate_panel = panel(gate_store)

time: 330 us -> 358 us (1.085)
  local copies, waits for them, and re-layouts: 0.23 us -> 74.3 us
  blocking collectives: 41.9 us -> 0 us
  waiting for transfers between devices: 193 us -> 180 us
  starting transfers between devices: 32 us -> 37.4 us
    unnamed x20 -> x63, local copies, waits for them, and re-layouts: 0.05 us -> 69.5 us
    all_to_all x1 -> x0, blocking collectives: 41.9 us -> none  [panel(): lax.all_to_all(store, 'expert', split_axis=0, concat_axis=1, tiled=True)[0]]
    all_to_all x3, waiting for transfers between devices: 138 us -> 113 us  [exchange(): return lax.all_to_all(a, 'expert', split_axis=0, concat_axis=0, tiled=True)]
    all_to_all x2 -> x3, waiting for transfers between devices: 51.8 us -> 63.7 us  [all_to_all(jnp.stack(jnp.split(a0, axis_size('expert'), 0), 0), 'expert',...]
    all_to_all x2 -> x3, starting transfers between devices: 10.4 us -> 15.7 us  [all_to_all(jnp.stack(jnp.split(a0, axis_size('expert'), 0), 0), 'expert',...]
    another operation x0 -> x3, local copies, waits for them, and re-layouts: none -> 4.63 us  [jnp.stack(jnp.split(a0, axis_size('expert'), 0), 0)]
  transfers between devices with their start and end apart: 9 -> 10, of which waited for: 6 -> 7; matrix products, arithmetic and copies ran while one was open for 14% -> 27% of each run, Pallas kernels for 0% -> 0%
where the time goes in v1:
time: 358 us; the launch traced here: 356 us
  waiting for transfers between devices  180 us (50%)
  local copies, waits for them, and re-layouts  74.3 us (21%)
  matrix products  61.8 us (17%)
  starting transfers between devices  37.4 us (10%)
    all_to_all x3, waiting for transfers between devices, exchange(): return lax.all_to_all(a, 'expert', split_axis=0, concat_axis=0, tiled=True)  113 us
    unnamed x63, local copies, waits for them, and re-layouts  69.5 us
    all_to_all x3, waiting for transfers between devices, all_to_all(jnp.stack(jnp.split(a0, axis_size('expert'), 0), 0), 'expert',...  63.7 us
    all_to_all x3, starting transfers between devices, all_to_all(jnp.stack(jnp.split(a0, axis_size('expert'), 0), 0), 'expert',...  15.7 us
    all_to_all x3, starting transfers between devices, exchange(): return lax.all_to_all(a, 'expert', split_axis=0, concat_axis=0, tiled=True)  14.4 us
    dot_general x1, matrix products, placed(): lax.dot_general(rows_in, up_grad, outer, preferred_element_type=f32)  8.14 us
    dot_general x1, matrix products, placed(): lax.dot_general(dy_rows, activation, outer, preferred_element_type=f32)  8.06 us
    dot_general x1, matrix products, placed(): up_pre = jnp.dot(rows_in, up_panel, preferred_element_type=f32)  8 us
  transfers between devices with their start and end apart: 10, of which 7 were waited for; matrix products, arithmetic and copies ran while one was open for 27% of the time, Pallas kernels for 0%

profile of v1, /device:TPU:15, one launch (start us, length us, event | category | flops | bytes accessed | tf_op | source)
XLA Modules:
  0.0 355.6 jit_solution(7723739133771676571)
XLA Ops:
  0.6 1.6 constant_dynamic-update-slice_fusion.47
  2.2 1.5 constant_dynamic-update-slice_fusion.46
  3.8 1.5 constant_dynamic-update-slice_fusion.45
  5.3 1.5 constant_dynamic-update-slice_fusion.44
  6.9 1.5 constant_dynamic-update-slice_fusion.43
  8.4 1.5 constant_dynamic-update-slice_fusion.42
  10.0 1.5 constant_dynamic-update-slice_fusion.41
  11.5 1.5 constant_dynamic-update-slice_fusion.40
  13.0 1.5 constant_dynamic-update-slice_fusion.39
  14.6 1.5 constant_dynamic-update-slice_fusion.38
  16.1 1.5 constant_dynamic-update-slice_fusion.37
  17.7 1.5 constant_dynamic-update-slice_fusion.36
  19.2 1.5 constant_dynamic-update-slice_fusion.35
  22.3 1.5 constant_dynamic-update-slice_fusion.33
  25.4 6.6 %all-to-all-start.4 = ((bf16[16,1,128,384]{3,2,1,0:T(8,128)(2,1)}), bf16[16,1,128,384]{3,2,1,0:T(8,128)(2,1)S(1)}, u32[]{:S(2)}, u32[]{:S(2)}) async-start(bf16[16,1,128,384]{3,2,1,0:T(8,128)(2,1)} %constant_dynamic-update-slice_fusion.32), calls=%async_computation.4 | async-start | bytes 3145728 | tf_op jit(solution)/shard_map/all_to_all | solution.py:8
  33.5 1.5 constant_dynamic-update-slice_fusion.30
  36.6 1.5 constant_dynamic-update-slice_fusion.28
  44.3 1.5 constant_dynamic-update-slice_fusion.23
  52.0 1.5 constant_dynamic-update-slice_fusion.18
  55.1 1.5 constant_dynamic-update-slice_fusion.16
  56.7 11.8 %all-to-all-done.4 = bf16[16,1,128,384]{3,2,1,0:T(8,128)(2,1)S(1)} async-done(((bf16[16,1,128,384]{3,2,1,0:T(8,128)(2,1)}), bf16[16,1,128,384]{3,2,1,0:T(8,128)(2,1)S(1)}, u32[]{:S(2)}, u32[]{:S(2)}) %all-to-all-start.4) | async-done | bytes 1572896 | tf_op jit(solution)/shard_map/all_to_all | solution.py:8
  68.4 4.6 %all-to-all-start.3 = ((bf16[16,1,128,384]{3,2,1,0:T(8,128)(2,1)}), bf16[16,1,128,384]{3,2,1,0:T(8,128)(2,1)}, u32[]{:S(2)}, u32[]{:S(2)}) async-start(bf16[16,1,128,384]{3,2,1,0:T(8,128)(2,1)} %constant_dynamic-update-slice_fusion.16), calls=%async_computation.3 | async-start | bytes 3145728 | tf_op jit(solution)/shard_map/all_to_all | solution.py:8
  73.5 2.2 convolution_convert_fusion
  75.7 33.6 %all-to-all-done.3 = bf16[16,1,128,384]{3,2,1,0:T(8,128)(2,1)} async-done(((bf16[16,1,128,384]{3,2,1,0:T(8,128)(2,1)}), bf16[16,1,128,384]{3,2,1,0:T(8,128)(2,1)}, u32[]{:S(2)}, u32[]{:S(2)}) %all-to-all-start.3) | async-done | bytes 1572896 | tf_op jit(solution)/shard_map/all_to_all | solution.py:8
  109.3 4.8 %all-to-all-start = ((bf16[16,72,1024]{2,1,0:T(8,128)(2,1)}), bf16[16,72,1024]{2,1,0:T(8,128)(2,1)}, u32[]{:S(2)}, u32[]{:S(2)}) async-start(bf16[16,72,1024]{2,1,0:T(8,128)(2,1)} %bitcast.2), calls=%async_computation | async-start | bytes 4718592 | tf_op jit(solution)/shard_map/all_to_all | solution.py:51
  114.6 2.2 fusion
  116.8 50.1 %all-to-all-done = bf16[16,72,1024]{2,1,0:T(8,128)(2,1)} async-done(((bf16[16,72,1024]{2,1,0:T(8,128)(2,1)}), bf16[16,72,1024]{2,1,0:T(8,128)(2,1)}, u32[]{:S(2)}, u32[]{:S(2)}) %all-to-all-start) | async-done | bytes 2359328 | tf_op jit(solution)/shard_map/all_to_all | solution.py:51
  167.0 4.6 %all-to-all-start.1 = ((bf16[16,72,1024]{2,1,0:T(8,128)(2,1)}), bf16[16,72,1024]{2,1,0:T(8,128)(2,1)}, u32[]{:S(2)}, u32[]{:S(2)}) async-start(bf16[16,72,1024]{2,1,0:T(8,128)(2,1)} %bitcast.5), calls=%async_computation.1 | async-start | bytes 4718592 | tf_op jit(solution)/shard_map/all_to_all | solution.py:51
  176.1 1.5 constant_dynamic-update-slice_fusion.12
  179.2 1.5 constant_dynamic-update-slice_fusion.10
  186.9 1.5 constant_dynamic-update-slice_fusion.5
  188.5 2.3 collective-permute-start
  190.8 1.5 constant_dynamic-update-slice_fusion.4
  198.5 25.9 %all-to-all-done.1 = bf16[16,72,1024]{2,1,0:T(8,128)(2,1)} async-done(((bf16[16,72,1024]{2,1,0:T(8,128)(2,1)}), bf16[16,72,1024]{2,1,0:T(8,128)(2,1)}, u32[]{:S(2)}, u32[]{:S(2)}) %all-to-all-start.1) | async-done | bytes 2359328 | tf_op jit(solution)/shard_map/all_to_all | solution.py:51
  224.5 4.6 %all-to-all-start.2 = ((bf16[16,1,128,384]{3,2,1,0:T(8,128)(2,1)}), bf16[16,1,128,384]{3,2,1,0:T(8,128)(2,1)}, u32[]{:S(2)}, u32[]{:S(2)}) async-start(bf16[16,1,128,384]{3,2,1,0:T(8,128)(2,1)} %constant_dynamic-update-slice_fusion), calls=%async_computation.2 | async-start | bytes 3145728 | tf_op jit(solution)/shard_map/all_to_all | solution.py:8
  229.0 2.3 collective-permute-start.1
  231.4 7.7 %fusion.29 = f32[1152,384]{1,0:T(8,128)} fusion(bf16[2048,384]{1,0:T(8,128)(2,1)S(1)} %bitcast.133, bf16[1152,1024]{1,0:T(8,128)(2,1)} %collective-permute-done, bf16[1152,1024]{1,0:T(8,128)(2,1)} %bitcast.3, pred[]{:T(512)S(6)} %eq.42), kind=kOutput, calls=%fused_computation.98 | convolution fusion | flops 1833172992 | bytes 8060929 | tf_op jit(solution)/shard_map/dot_general | solution.py:63
  239.0 8.0 %fusion.30 = f32[1152,384]{1,0:T(8,128)} fusion(bf16[2048,384]{1,0:T(8,128)(2,1)} %bitcast.40, bf16[1152,1024]{1,0:T(8,128)(2,1)} %collective-permute-done, bf16[1152,1024]{1,0:T(8,128)(2,1)} %bitcast.3, pred[]{:T(512)S(6)} %eq.42), kind=kOutput, calls=%fused_computation.99 | convolution fusion | flops 1833172992 | bytes 8060929 | tf_op jit(solution)/shard_map/dot_general | solution.py:64
  247.0 18.2 %all-to-all-done.2 = bf16[16,1,128,384]{3,2,1,0:T(8,128)(2,1)} async-done(((bf16[16,1,128,384]{3,2,1,0:T(8,128)(2,1)}), bf16[16,1,128,384]{3,2,1,0:T(8,128)(2,1)}, u32[]{:S(2)}, u32[]{:S(2)}) %all-to-all-start.2) | async-done | bytes 1572896 | tf_op jit(solution)/shard_map/all_to_all | solution.py:8
  265.3 7.4 %multiply_convert_fusion.1 = (bf16[1152,384]{1,0:T(8,128)(2,1)S(1)}, bf16[1152,384]{1,0:T(8,128)(2,1)S(1)}) fusion(f32[1152,384]{1,0:T(8,128)} %fusion.29, f32[1152,384]{1,0:T(8,128)} %fusion.30, bf16[2048,384]{1,0:T(8,128)(2,1)} %bitcast.23, bf16[1152,1024]{1,0:T(8,128)(2,1)} %collective-permute-done.1, bf16[1152,1024]{1,0:T(8,128)(2,1)} %bitcast.6, ...), kind=kOutput, calls=%fused_computation.16 | convolution fusion | flops 1838923776 | bytes 11599873 | tf_op jit(solution)/shard_map/dot_general | solution.py:67
  274.2 2.6 fusion.1
  279.4 2.7 collective-permute-done.2
  282.1 4.0 %add_convert_fusion = bf16[1152,1024]{1,0:T(8,128)(2,1)} fusion(bf16[1152,1024]{1,0:T(8,128)(2,1)S(1)} %collective-permute-done.2, f32[1152,1024]{1,0:T(8,128)S(1)} %fusion.14, bf16[1152,384]{1,0:T(8,128)(2,1)S(1)} %get-tuple-element.4, bf16[2048,384]{1,0:T(8,128)(2,1)} %bitcast.40, s32[]{:T(128)S(6)} %select_n.45), kind=kOutput, calls=%fused_computation.5 | convolution fusion | flops 910688256 | bytes 11108356 | tf_op jit(solution)/shard_map/dot_general | solution.py:76
  286.1 5.1 %all-to-all-start.5 = ((bf16[16,72,1024]{2,1,0:T(8,128)(2,1)}), bf16[16,72,1024]{2,1,0:T(8,128)(2,1)S(1)}, u32[]{:S(2)}, u32[]{:S(2)}) async-start(bf16[16,72,1024]{2,1,0:T(8,128)(2,1)} %bitcast.132), calls=%async_computation.5 | async-start | bytes 4718592 | tf_op jit(solution)/shard_map/all_to_all | solution.py:51
  291.2 8.1 %fusion.3 = bf16[1,2048,384]{2,1,0:T(8,128)(2,1)} fusion(bf16[1152,384]{1,0:T(8,128)(2,1)} %copy-done.3, bf16[1152,1024]{1,0:T(8,128)(2,1)} %collective-permute-done, bf16[1152,1024]{1,0:T(8,128)(2,1)} %bitcast.3, pred[]{:T(512)S(6)} %eq.42), kind=kOutput, calls=%fused_computation.13 | convolution fusion | flops 1833959424 | bytes 7176193 | tf_op jit(solution)/shard_map/dot_general | solution.py:88
  299.4 8.1 %fusion.4 = bf16[1,2048,384]{2,1,0:T(8,128)(2,1)} fusion(f32[1152,384]{1,0:T(8,128)S(1)} %copy-done.8, f32[1152,384]{1,0:T(8,128)S(1)} %copy-done.7, bf16[1152,1024]{1,0:T(8,128)(2,1)} %collective-permute-done.1, bf16[1152,1024]{1,0:T(8,128)(2,1)} %bitcast.6, pred[]{:T(512)S(6)} %eq.42), kind=kOutput, calls=%fused_computation.14 | convolution fusion | flops 1836613632 | bytes 9830401 | tf_op jit(solution)/shard_map/dot_general | solution.py:86
  307.5 37.3 %all-to-all-done.5 = bf16[16,72,1024]{2,1,0:T(8,128)(2,1)S(1)} async-done(((bf16[16,72,1024]{2,1,0:T(8,128)(2,1)}), bf16[16,72,1024]{2,1,0:T(8,128)(2,1)S(1)}, u32[]{:S(2)}, u32[]{:S(2)}) %all-to-all-start.5) | async-done | bytes 2359328 | tf_op jit(solution)/shard_map/all_to_all | solution.py:51
  346.8 7.8 %fusion.2 = bf16[1,2048,384]{2,1,0:T(8,128)(2,1)} fusion(bf16[1152,384]{1,0:T(8,128)(2,1)S(1)} %copy-done.2, bf16[1152,1024]{1,0:T(8,128)(2,1)} %collective-permute-done, bf16[1152,1024]{1,0:T(8,128)(2,1)} %bitcast.3, pred[]{:T(512)S(6)} %eq.42), kind=kOutput, calls=%fused_computation.12 | convolution fusion | flops 1833959424 | bytes 7176193 | tf_op jit(solution)/shard_map/dot_general | solution.py:87
  (60 shorter events, 46.5 us)
Async XLA Ops:
  0.6 72.9 %copy-start = (bf16[128,2048]{1,0:T(8,128)(2,1)S(1)}, bf16[128,2048]{1,0:T(8,128)(2,1)}, u32[]{:S(2)}) copy-start(bf16[128,2048]{1,0:T(8,128)(2,1)} %param.7) | copy-start | bytes 1572868
  25.4 43.1 %all-to-all-start.4 = ((bf16[16,1,128,384]{3,2,1,0:T(8,128)(2,1)}), bf16[16,1,128,384]{3,2,1,0:T(8,128)(2,1)S(1)}, u32[]{:S(2)}, u32[]{:S(2)}) async-start(bf16[16,1,128,384]{3,2,1,0:T(8,128)(2,1)} %constant_dynamic-update-slice_fusion.32), calls=%async_computation.4 | async-start | bytes 3145728 | tf_op jit(solution)/shard_map/all_to_all | solution.py:8
  56.6 16.4 %copy-start.5 = (s32[128,8]{0,1:T(8,128)S(1)}, s32[128,8]{0,1:T(8,128)}, u32[]{:S(2)}) copy-start(s32[128,8]{0,1:T(8,128)} %param.9) | copy-start | bytes 12292
  68.4 40.9 %all-to-all-start.3 = ((bf16[16,1,128,384]{3,2,1,0:T(8,128)(2,1)}), bf16[16,1,128,384]{3,2,1,0:T(8,128)(2,1)}, u32[]{:S(2)}, u32[]{:S(2)}) async-start(bf16[16,1,128,384]{3,2,1,0:T(8,128)(2,1)} %constant_dynamic-update-slice_fusion.16), calls=%async_computation.3 | async-start | bytes 3145728 | tf_op jit(solution)/shard_map/all_to_all | solution.py:8
  109.3 4.8 %copy-start.6 = (f32[128,8]{0,1:T(8,128)S(1)}, f32[128,8]{0,1:T(8,128)}, u32[]{:S(2)}) copy-start(f32[128,8]{0,1:T(8,128)} %param.10) | copy-start | bytes 12292
  109.3 5.2 %copy-start.4 = (bf16[128,2048]{1,0:T(8,128)(2,1)S(1)}, bf16[128,2048]{1,0:T(8,128)(2,1)}, u32[]{:S(2)}) copy-start(bf16[128,2048]{1,0:T(8,128)(2,1)} %param.8) | copy-start | bytes 1572868
  109.3 57.6 %all-to-all-start = ((bf16[16,72,1024]{2,1,0:T(8,128)(2,1)}), bf16[16,72,1024]{2,1,0:T(8,128)(2,1)}, u32[]{:S(2)}, u32[]{:S(2)}) async-start(bf16[16,72,1024]{2,1,0:T(8,128)(2,1)} %bitcast.2), calls=%async_computation | async-start | bytes 4718592 | tf_op jit(solution)/shard_map/all_to_all | solution.py:51
  167.0 57.5 %all-to-all-start.1 = ((bf16[16,72,1024]{2,1,0:T(8,128)(2,1)}), bf16[16,72,1024]{2,1,0:T(8,128)(2,1)}, u32[]{:S(2)}, u32[]{:S(2)}) async-start(bf16[16,72,1024]{2,1,0:T(8,128)(2,1)} %bitcast.5), calls=%async_computation.1 | async-start | bytes 4718592 | tf_op jit(solution)/shard_map/all_to_all | solution.py:51
  188.5 42.9 %collective-permute-start = (bf16[1152,1024]{1,0:T(8,128)(2,1)}, bf16[1152,1024]{1,0:T(8,128)(2,1)}, u32[]{:S(2)}, u32[]{:S(2)}) collective-permute-start(bf16[1152,1024]{1,0:T(8,128)(2,1)} %bitcast.3), channel_id=1, source_target_pairs={{0,16},{16,0},{1,17},{17,1},{2,18},{18,2},{3,19},{19,3},{4,20},{20... | collective-permute-start | bytes 7077896 | tf_op jit(solution)/shard_map/ppermute | solution.py:18
  224.5 40.8 %all-to-all-start.2 = ((bf16[16,1,128,384]{3,2,1,0:T(8,128)(2,1)}), bf16[16,1,128,384]{3,2,1,0:T(8,128)(2,1)}, u32[]{:S(2)}, u32[]{:S(2)}) async-start(bf16[16,1,128,384]{3,2,1,0:T(8,128)(2,1)} %constant_dynamic-update-slice_fusion), calls=%async_computation.2 | async-start | bytes 3145728 | tf_op jit(solution)/shard_map/all_to_all | solution.py:8
  229.0 36.3 %collective-permute-start.1 = (bf16[1152,1024]{1,0:T(8,128)(2,1)}, bf16[1152,1024]{1,0:T(8,128)(2,1)}, u32[]{:S(2)}, u32[]{:S(2)}) collective-permute-start(bf16[1152,1024]{1,0:T(8,128)(2,1)} %bitcast.6), channel_id=1, source_target_pairs={{0,16},{16,0},{1,17},{17,1},{2,18},{18,2},{3,19},{19,3},{4,20},{20... | collective-permute-start | bytes 7077896 | tf_op jit(solution)/shard_map/ppermute | solution.py:18
  272.7 5.2 %copy-start.1 = (bf16[1152,384]{1,0:T(8,128)(2,1)}, bf16[1152,384]{1,0:T(8,128)(2,1)S(1)}, u32[]{:S(2)}) copy-start(bf16[1152,384]{1,0:T(8,128)(2,1)S(1)} %get-tuple-element.5) | copy-start | bytes 2654212
  272.7 9.4 %copy-start.3 = (bf16[1152,384]{1,0:T(8,128)(2,1)}, bf16[1152,384]{1,0:T(8,128)(2,1)S(1)}, u32[]{:S(2)}) copy-start(bf16[1152,384]{1,0:T(8,128)(2,1)S(1)} %get-tuple-element.4) | copy-start | bytes 2654212
  276.8 5.3 %collective-permute-start.2 = (bf16[1152,1024]{1,0:T(8,128)(2,1)S(1)}, bf16[1152,1024]{1,0:T(8,128)(2,1)S(1)}, u32[]{:S(2)}, u32[]{:S(2)}) collective-permute-start(bf16[1152,1024]{1,0:T(8,128)(2,1)S(1)} %fusion.1), channel_id=1, source_target_pairs={{0,16},{16,0},{1,17},{17,1},{2,18},{18,2},{3,19},{19,3},{4,20},{20... | collective-permute-start | bytes 7077896 | tf_op jit(solution)/shard_map/ppermute | solution.py:18
  286.1 58.6 %all-to-all-start.5 = ((bf16[16,72,1024]{2,1,0:T(8,128)(2,1)}), bf16[16,72,1024]{2,1,0:T(8,128)(2,1)S(1)}, u32[]{:S(2)}, u32[]{:S(2)}) async-start(bf16[16,72,1024]{2,1,0:T(8,128)(2,1)} %bitcast.132), calls=%async_computation.5 | async-start | bytes 4718592 | tf_op jit(solution)/shard_map/all_to_all | solution.py:51
  291.2 8.2 %copy-start.7 = (f32[1152,384]{1,0:T(8,128)S(1)}, f32[1152,384]{1,0:T(8,128)}, u32[]{:S(2)}) copy-start(f32[1152,384]{1,0:T(8,128)} %fusion.29) | copy-start | bytes 5308420
  291.2 8.2 %copy-start.8 = (f32[1152,384]{1,0:T(8,128)S(1)}, f32[1152,384]{1,0:T(8,128)}, u32[]{:S(2)}) copy-start(f32[1152,384]{1,0:T(8,128)} %fusion.30) | copy-start | bytes 5308420
  344.8 2.0 copy-start.2
  345.4 9.3 %collective-permute-start.3 = (bf16[128,1024]{1,0:T(8,128)(2,1)S(1)}, bf16[128,1024]{1,0:T(8,128)(2,1)S(1)}, u32[]{:S(2)}, u32[]{:S(2)}) collective-permute-start(bf16[128,1024]{1,0:T(8,128)(2,1)S(1)} %fusion.5), channel_id=1, source_target_pairs={{0,16},{16,0},{1,17},{17,1},{2,18},{18,2},{3,19},{19,3},{4,20},{20... | collective-permute-start | bytes 786440 | tf_op jit(solution)/shard_map/ppermute | solution.py:18
